TPU v7x, 32 devices: a whole 2x2x4 slice. The times are simulated.
32 devices in a mesh: vec: 8 (over z, core), rep: 4 (over y, x).
Axes of the slice: x: 2, y: 2, z: 4, core: 2. Of those that a mesh axis runs over, the one named last changes fastest.
Arguments:
- vectors: bfloat16 [1024, 1024], P('vec'), may hold values from 0 to 2
- pivot_index: int32 [4, 8], P('rep'), may hold values from 0 to 1023
Outputs:
- similarity: bfloat16 [7, 32, 1024, 128], P(None, 'rep', 'vec')
All inputs are finite; a program needn't handle non-finite values.
Results may differ from a plain program's by a relative error of at most 0.011.
Values may be sent and summed in bfloat16 or wider, within the bound.
A program may use at most 64 MiB of HBM per device.

v0:
```python
import math
import jax
import jax.numpy as jnp
from jax import lax
from jax.sharding import PartitionSpec as P

HALF = 3


def from_behind(block, axis, distance):
    devices = range(lax.axis_size(axis))
    route = [((i - distance) % len(devices), i) for i in devices]
    return lax.ppermute(block, axis, route)


def contract(left, right):
    return lax.dot_general(
        left, right, (((1,), (1,)), ((), ())), preferred_element_type=jnp.float32
    )


def on_device(vectors, pivot_index):
    block_rows, fields = vectors.shape
    position = lax.axis_index("vec")
    wanted = pivot_index.reshape(-1) - position * block_rows
    columns = jnp.arange(block_rows, dtype=jnp.int32)
    onehot = (wanted[:, None] == columns[None, :]).astype(jnp.bfloat16)
    local_rows = jnp.dot(onehot, vectors, preferred_element_type=jnp.float32)
    pivots = lax.psum(local_rows, "vec")
    count = pivots.shape[0]
    centre = jnp.sum(pivots, axis=1) / fields
    scaled = (vectors.astype(jnp.float32)[None, :, :] * pivots[:, None, :]).astype(jnp.bfloat16)
    scaled = scaled.reshape(count * block_rows, fields)
    replicas = lax.axis_size("rep")
    share = block_rows // replicas
    own_rows = lax.dynamic_slice_in_dim(vectors, lax.axis_index("rep") * share, share, 0)
    window = 2 * HALF + 1
    triples = [None] * window
    grams = [None] * window
    triples[HALF] = contract(scaled, vectors)
    grams[HALF] = contract(own_rows, vectors)
    lower = vectors
    upper = vectors
    for reach in range(1, HALF + 1):
        lower = from_behind(lower, "vec", 1)
        upper = from_behind(upper, "vec", -1)
        triples[HALF - reach] = contract(scaled, lower)
        grams[HALF - reach] = contract(own_rows, lower)
        triples[HALF + reach] = contract(scaled, upper)
        grams[HALF + reach] = contract(own_rows, upper)
    triple_all = jnp.stack(triples).reshape(window, count, block_rows, block_rows)
    gram_all = jnp.stack(grams)
    gram_all = lax.all_gather(gram_all, "rep", axis=1, tiled=True)
    similarity = (triple_all - centre[None, :, None, None] * gram_all[:, None, :, :]) / math.sqrt(
        fields
    )
    return similarity.astype(jnp.bfloat16)


def solution(mesh):
    in_specs = (P("vec", None), P("rep", None))
    out_specs = P(None, "rep", "vec", None)
    return jax.shard_map(
        on_device, mesh=mesh, in_specs=in_specs, out_specs=out_specs, check_vma=False
    )
```

profile of v0, /device:TPU:0, one launch (start us, length us, event | category | flops | bytes accessed | tf_op | source)
XLA Modules:
  0.0 71.4 jit_solution(5123657337619987184)
XLA Ops:
  0.0 0.5 collective-permute-start
  0.5 4.0 %collective-permute-start.3 = (bf16[128,1024]{1,0:T(8,128)(2,1)}, bf16[128,1024]{1,0:T(8,128)(2,1)S(1)}, u32[]{:S(2)}, u32[]{:S(2)}) collective-permute-start(bf16[128,1024]{1,0:T(8,128)(2,1)} %param.2), channel_id=1, source_target_pairs={{4,0},{8,4},{12,8},{16,12},{20,16},{24,20},{28,24},{0,28},{5,1},{9... | collective-permute-start | bytes 786440 | tf_op jit(solution)/shard_map/ppermute | solution.py:13
  4.5 4.5 %collective-permute-done = bf16[128,1024]{1,0:T(8,128)(2,1)S(1)} collective-permute-done((bf16[128,1024]{1,0:T(8,128)(2,1)}, bf16[128,1024]{1,0:T(8,128)(2,1)S(1)}, u32[]{:S(2)}, u32[]{:S(2)}) %collective-permute-start) | collective-permute-done | bytes 262176 | tf_op jit(solution)/shard_map/ppermute | solution.py:13
  9.0 0.0 collective-permute-start.1
  9.0 0.7 subtract_bitcast_fusion
  9.7 0.0 collective-permute-done.3
  9.7 3.5 %collective-permute-start.4 = (bf16[128,1024]{1,0:T(8,128)(2,1)S(1)}, bf16[128,1024]{1,0:T(8,128)(2,1)S(1)}, u32[]{:S(2)}, u32[]{:S(2)}) collective-permute-start(bf16[128,1024]{1,0:T(8,128)(2,1)S(1)} %collective-permute-done.3), channel_id=1, source_target_pairs={{4,0},{8,4},{12,8},{16,12},{20,16},{24,20},{28,24},{0,28},{5,1},{9... | collective-permute-start | bytes 786440 | tf_op jit(solution)/shard_map/ppermute | solution.py:13
  13.2 3.5 %collective-permute-done.1 = bf16[128,1024]{1,0:T(8,128)(2,1)S(1)} collective-permute-done((bf16[128,1024]{1,0:T(8,128)(2,1)S(1)}, bf16[128,1024]{1,0:T(8,128)(2,1)S(1)}, u32[]{:S(2)}, u32[]{:S(2)}) %collective-permute-start.1) | collective-permute-done | bytes 262176 | tf_op jit(solution)/shard_map/ppermute | solution.py:13
  16.7 0.0 collective-permute-start.2
  16.7 1.1 %fusion.56 = f32[8,1024]{1,0:T(8,128)S(1)} fusion(bf16[128,1024]{1,0:T(8,128)(2,1)} %param.2, s32[8]{0:T(128)S(1)} %subtract_bitcast_fusion), kind=kOutput, calls=%fused_computation.66 | convolution fusion | flops 2098176 | bytes 294944 | tf_op jit(solution)/shard_map/dot_general | solution.py:28
  17.8 1.0 %convert_element_type.21 = f32[128,1024]{1,0:T(8,128)S(1)} convert(bf16[128,1024]{1,0:T(8,128)(2,1)} %param.2) | non-fusion elementwise | flops 131072 | bytes 786432 | tf_op jit(solution)/shard_map/convert_element_type | solution.py:32
  18.8 29.4 %psum.7 = f32[8,1024]{1,0:T(8,128)S(1)} all-reduce(f32[8,1024]{1,0:T(8,128)S(1)} %fusion.56), channel_id=1, replica_groups=mesh['vec'=8,'rep'=4] {'vec'}, use_global_device_ids=true, to_apply=%region_0.0 | all-reduce | flops 8192 | bytes 65536 | tf_op jit(solution)/shard_map/psum | solution.py:29
  48.3 0.1 reduce_sum.9
  48.4 0.0 collective-permute-done.4
  48.4 0.1 collective-permute-start.5
  48.5 0.0 collective-permute-done.2
  48.5 1.0 %fusion.41 = f32[7,32,128]{2,1,0:T(8,128)S(1)} fusion(bf16[128,1024]{1,0:T(8,128)(2,1)S(1)} %collective-permute-done.2, bf16[128,1024]{1,0:T(8,128)(2,1)} %param.2, s32[]{:T(128)S(6)} %select_n.3), kind=kOutput, calls=%fused_computation.50 | convolution fusion | flops 8388607 | bytes 344068 | tf_op jit(solution)/shard_map/dot_general | solution.py:17
  49.5 1.0 %fusion.40 = f32[7,32,128]{2,1,0:T(8,128)S(1)} fusion(f32[7,32,128]{2,1,0:T(8,128)S(1)} %fusion.41, bf16[128,1024]{1,0:T(8,128)(2,1)S(1)} %collective-permute-done.1, bf16[128,1024]{1,0:T(8,128)(2,1)} %param.2, s32[]{:T(128)S(6)} %select_n.3), kind=kOutput, calls=%fused_computation.48 | convolution fusion | flops 8388608 | bytes 344068 | tf_op jit(solution)/shard_map/dot_general | solution.py:17
  50.5 1.0 %fusion.39 = f32[7,32,128]{2,1,0:T(8,128)S(1)} fusion(f32[7,32,128]{2,1,0:T(8,128)S(1)} %fusion.40, bf16[128,1024]{1,0:T(8,128)(2,1)S(1)} %collective-permute-done, bf16[128,1024]{1,0:T(8,128)(2,1)} %param.2, s32[]{:T(128)S(6)} %select_n.3), kind=kOutput, calls=%fused_computation.46 | convolution fusion | flops 8388608 | bytes 344068 | tf_op jit(solution)/shard_map/dot_general | solution.py:17
  51.6 1.2 %fusion.38 = f32[7,32,128]{2,1,0:T(8,128)S(1)} fusion(f32[7,32,128]{2,1,0:T(8,128)S(1)} %fusion.39, bf16[128,1024]{1,0:T(8,128)(2,1)} %param.2, s32[]{:T(128)S(6)} %select_n.3), kind=kOutput, calls=%fused_computation.44 | convolution fusion | flops 8388608 | bytes 344068 | tf_op jit(solution)/shard_map/dot_general | solution.py:17
  52.8 0.0 copy-start
  52.8 0.7 %fusion.22 = f32[7,8,128,128]{3,2,1,0:T(8,128)S(1)} fusion(f32[8,1024]{1,0:T(8,128)S(1)} %psum.7, f32[128,1024]{1,0:T(8,128)S(1)} %convert_element_type.21, bf16[128,1024]{1,0:T(8,128)(2,1)S(1)} %collective-permute-done.2), kind=kOutput, calls=%fused_computation.24 | convolution fusion | flops 270532608 | bytes 1343488 | tf_op jit(solution)/shard_map/dot_general | solution.py:17
  53.6 0.7 fusion.24
  54.3 0.7 fusion.26
  55.0 0.0 copy-done
  55.0 0.2 fusion.37
  55.2 0.2 fusion.36
  55.4 0.7 %fusion.28 = f32[7,8,128,128]{3,2,1,0:T(8,128)S(1)} fusion(f32[7,8,128,128]{3,2,1,0:T(8,128)S(1)} %fusion.26, f32[8,1024]{1,0:T(8,128)S(1)} %psum.7, f32[128,1024]{1,0:T(8,128)S(1)} %convert_element_type.21, bf16[128,1024]{1,0:T(8,128)(2,1)S(1)} %copy-done), kind=kOutput, calls=%fused_computation.30 | convolution fusion | flops 270532608 | bytes 1343488 | tf_op jit(solution)/shard_map/dot_general | solution.py:17
  56.1 0.0 collective-permute-done.5
  56.1 0.2 fusion.35
  56.3 11.0 %all_gather.3 = f32[7,128,128]{2,1,0:T(8,128)S(1)} all-gather(f32[7,32,128]{2,1,0:T(8,128)S(1)} %fusion.35), channel_id=1, replica_groups=mesh['vec'=8,'rep'=4] {'rep'}, dimensions={1}, use_global_device_ids=true | all-gather | bytes 573440 | tf_op jit(solution)/shard_map/all_gather | solution.py:53
  67.3 0.7 fusion.30
  68.0 0.7 fusion.32
  68.8 0.7 fusion.34
  69.5 1.9 %multiply_convert_fusion.8 = bf16[7,8,128,128]{3,2,1,0:T(8,128)(2,1)} fusion(f32[7,8,128,128]{3,2,1,0:T(8,128)S(1)} %fusion.34, f32[7,128,128]{2,1,0:T(8,128)S(1)} %all_gather.3, f32[8]{0:T(128)S(1)} %broadcast_multiply_fusion), kind=kLoop, calls=%fused_computation.8 | loop fusion | flops 3670016 | bytes 5963808 | tf_op jit(solution)/shard_map/convert_element_type | solution.py:57
  (1 shorter events, 0.0 us)
Async XLA Ops:
  0.0 9.0 %collective-permute-start = (bf16[128,1024]{1,0:T(8,128)(2,1)}, bf16[128,1024]{1,0:T(8,128)(2,1)S(1)}, u32[]{:S(2)}, u32[]{:S(2)}) collective-permute-start(bf16[128,1024]{1,0:T(8,128)(2,1)} %param.2), channel_id=1, source_target_pairs={{28,0},{0,4},{4,8},{8,12},{12,16},{16,20},{20,24},{24,28},{29,1},{... | collective-permute-start | bytes 786440 | tf_op jit(solution)/shard_map/ppermute | solution.py:13
  0.5 9.2 %collective-permute-start.3 = (bf16[128,1024]{1,0:T(8,128)(2,1)}, bf16[128,1024]{1,0:T(8,128)(2,1)S(1)}, u32[]{:S(2)}, u32[]{:S(2)}) collective-permute-start(bf16[128,1024]{1,0:T(8,128)(2,1)} %param.2), channel_id=1, source_target_pairs={{4,0},{8,4},{12,8},{16,12},{20,16},{24,20},{28,24},{0,28},{5,1},{9... | collective-permute-start | bytes 786440 | tf_op jit(solution)/shard_map/ppermute | solution.py:13
  9.0 7.7 %collective-permute-start.1 = (bf16[128,1024]{1,0:T(8,128)(2,1)S(1)}, bf16[128,1024]{1,0:T(8,128)(2,1)S(1)}, u32[]{:S(2)}, u32[]{:S(2)}) collective-permute-start(bf16[128,1024]{1,0:T(8,128)(2,1)S(1)} %collective-permute-done), channel_id=1, source_target_pairs={{28,0},{0,4},{4,8},{8,12},{12,16},{16,20},{20,24},{24,28},{29,1},{... | collective-permute-start | bytes 786440 | tf_op jit(solution)/shard_map/ppermute | solution.py:13
  9.7 38.7 %collective-permute-start.4 = (bf16[128,1024]{1,0:T(8,128)(2,1)S(1)}, bf16[128,1024]{1,0:T(8,128)(2,1)S(1)}, u32[]{:S(2)}, u32[]{:S(2)}) collective-permute-start(bf16[128,1024]{1,0:T(8,128)(2,1)S(1)} %collective-permute-done.3), channel_id=1, source_target_pairs={{4,0},{8,4},{12,8},{16,12},{20,16},{24,20},{28,24},{0,28},{5,1},{9... | collective-permute-start | bytes 786440 | tf_op jit(solution)/shard_map/ppermute | solution.py:13
  16.7 31.8 %collective-permute-start.2 = (bf16[128,1024]{1,0:T(8,128)(2,1)S(1)}, bf16[128,1024]{1,0:T(8,128)(2,1)S(1)}, u32[]{:S(2)}, u32[]{:S(2)}) collective-permute-start(bf16[128,1024]{1,0:T(8,128)(2,1)S(1)} %collective-permute-done.1), channel_id=1, source_target_pairs={{28,0},{0,4},{4,8},{8,12},{12,16},{16,20},{20,24},{24,28},{29,1},{... | collective-permute-start | bytes 786440 | tf_op jit(solution)/shard_map/ppermute | solution.py:13
  48.4 7.7 %collective-permute-start.5 = (bf16[128,1024]{1,0:T(8,128)(2,1)S(1)}, bf16[128,1024]{1,0:T(8,128)(2,1)S(1)}, u32[]{:S(2)}, u32[]{:S(2)}) collective-permute-start(bf16[128,1024]{1,0:T(8,128)(2,1)S(1)} %collective-permute-done.4), channel_id=1, source_target_pairs={{4,0},{8,4},{12,8},{16,12},{20,16},{24,20},{28,24},{0,28},{5,1},{9... | collective-permute-start | bytes 786440 | tf_op jit(solution)/shard_map/ppermute | solution.py:13
  52.8 2.2 %copy-start = (bf16[128,1024]{1,0:T(8,128)(2,1)S(1)}, bf16[128,1024]{1,0:T(8,128)(2,1)}, u32[]{:S(2)}) copy-start(bf16[128,1024]{1,0:T(8,128)(2,1)} %param.2) | copy-start | bytes 786436
where the time goes:
time: 71.7 us; the launch traced here: 71.4 us
  blocking collectives  40.5 us (56%)
  matrix products  11 us (15%)
  starting transfers between devices  8.13 us (11%)
  waiting for transfers between devices  7.96 us (11%)
  other arithmetic  3.69 us (5%)
    psum x1, blocking collectives, on_device(): pivots = lax.psum(local_rows, 'vec')  29.4 us
    all_gather x1, blocking collectives, on_device(): gram_all = lax.all_gather(gram_all, 'rep', axis=1, tiled=True)  11 us
    dot_general x14, matrix products, contract(): lax.dot_general(left, right, (((1,), (1,)), ((), ())), preferred_element_...  9.87 us
    ppermute x6, starting transfers between devices, from_behind(): return lax.ppermute(block, axis, route)  8.13 us
    ppermute x6, waiting for transfers between devices, from_behind(): return lax.ppermute(block, axis, route)  7.96 us
    convert_element_type x1, other arithmetic, on_device(): return similarity.astype(jnp.bfloat16)  1.9 us
  transfers between devices with their start and end apart: 6, of which 2 were waited for; matrix products, arithmetic and copies ran while one was open for 15% of the time, Pallas kernels for 0%

commit v1 on v0

--- a/solution.py
+++ b/solution.py
@@ -26,7 +26,9 @@
     columns = jnp.arange(block_rows, dtype=jnp.int32)
     onehot = (wanted[:, None] == columns[None, :]).astype(jnp.bfloat16)
     local_rows = jnp.dot(onehot, vectors, preferred_element_type=jnp.float32)
-    pivots = lax.psum(local_rows, "vec")
+    pivots = local_rows
+    for hop in (1, 2, 4):
+        pivots = pivots + lax.ppermute(pivots, "vec", [(dev, dev ^ hop) for dev in range(8)])
     count = pivots.shape[0]
     centre = jnp.sum(pivots, axis=1) / fields
     scaled = (vectors.astype(jnp.float32)[None, :, :] * pivots[:, None, :]).astype(jnp.bfloat16)

time: 71.7 us -> 54 us (0.75)
  blocking collectives: 40.5 us -> 9.8 us
  starting transfers between devices: 8.13 us -> 16.3 us
  waiting for transfers between devices: 7.96 us -> 12.6 us
    psum x1 -> x0, blocking collectives: 29.4 us -> none  [on_device(): pivots = lax.psum(local_rows, 'vec')]
    ppermute x0 -> x3, starting transfers between devices: none -> 7.6 us  [on_device(): lax.ppermute(pivots, 'vec', [(dev, dev ^ hop) for dev in range(8)])]
    ppermute x0 -> x3, waiting for transfers between devices: none -> 3.07 us  [on_device(): lax.ppermute(pivots, 'vec', [(dev, dev ^ hop) for dev in range(8)])]
    ppermute x6, waiting for transfers between devices: 7.96 us -> 9.57 us  [from_behind(): return lax.ppermute(block, axis, route)]
    all_gather x1, blocking collectives: 11 us -> 9.8 us  [on_device(): gram_all = lax.all_gather(gram_all, 'rep', axis=1, tiled=True)]
  transfers between devices with their start and end apart: 6 -> 9, of which waited for: 2 -> 5; matrix products, arithmetic and copies ran while one was open for 15% -> 20% of each run, Pallas kernels for 0% -> 0%
where the time goes in v1:
time: 54 us; the launch traced here: 53.6 us
  starting transfers between devices  16.3 us (30%)
  waiting for transfers between devices  12.6 us (23%)
  matrix products  11 us (20%)
  blocking collectives  9.8 us (18%)
  other arithmetic  3.69 us (7%)
    dot_general x14, matrix products, contract(): lax.dot_general(left, right, (((1,), (1,)), ((), ())), preferred_element_...  9.87 us
    all_gather x1, blocking collectives, on_device(): gram_all = lax.all_gather(gram_all, 'rep', axis=1, tiled=True)  9.8 us
    ppermute x6, waiting for transfers between devices, from_behind(): return lax.ppermute(block, axis, route)  9.57 us
    ppermute x6, starting transfers between devices, from_behind(): return lax.ppermute(block, axis, route)  8.75 us
    ppermute x3, starting transfers between devices, on_device(): lax.ppermute(pivots, 'vec', [(dev, dev ^ hop) for dev in range(8)])  7.6 us
    ppermute x3, waiting for transfers between devices, on_device(): lax.ppermute(pivots, 'vec', [(dev, dev ^ hop) for dev in range(8)])  3.07 us
    convert_element_type x1, other arithmetic, on_device(): return similarity.astype(jnp.bfloat16)  1.9 us
    dot_general x1, matrix products, on_device(): local_rows = jnp.dot(onehot, vectors, preferred_element_type=jnp.float32)  1.14 us
  transfers between devices with their start and end apart: 9, of which 5 were waited for; matrix products, arithmetic and copies ran while one was open for 20% of the time, Pallas kernels for 0%

profile of v1, /device:TPU:0, one launch (start us, length us, event | category | flops | bytes accessed | tf_op | source)
XLA Modules:
  0.0 53.6 jit_solution(14228635972462127360)
XLA Ops:
  0.0 0.5 collective-permute-start.3
  0.5 4.0 %collective-permute-start.6 = (bf16[128,1024]{1,0:T(8,128)(2,1)}, bf16[128,1024]{1,0:T(8,128)(2,1)S(1)}, u32[]{:S(2)}, u32[]{:S(2)}) collective-permute-start(bf16[128,1024]{1,0:T(8,128)(2,1)} %param.2), channel_id=1, source_target_pairs={{4,0},{8,4},{12,8},{16,12},{20,16},{24,20},{28,24},{0,28},{5,1},{9... | collective-permute-start | bytes 786440 | tf_op jit(solution)/shard_map/ppermute | solution.py:13
  4.5 0.7 %subtract_bitcast_fusion = s32[8]{0:T(128)S(1)} fusion(s32[1,8]{1,0:T(1,128)} %param.3, s32[]{:T(128)S(6)} %mul.44), kind=kLoop, calls=%fused_computation.68 | loop fusion | flops 8 | bytes 68 | tf_op jit(solution)/shard_map/sub | solution.py:25
  5.2 3.8 %collective-permute-done.3 = bf16[128,1024]{1,0:T(8,128)(2,1)S(1)} collective-permute-done((bf16[128,1024]{1,0:T(8,128)(2,1)}, bf16[128,1024]{1,0:T(8,128)(2,1)S(1)}, u32[]{:S(2)}, u32[]{:S(2)}) %collective-permute-start.3) | collective-permute-done | bytes 262176 | tf_op jit(solution)/shard_map/ppermute | solution.py:13
  9.0 0.0 collective-permute-start.4
  9.0 1.1 %fusion.56 = f32[8,1024]{1,0:T(8,128)S(1)} fusion(bf16[128,1024]{1,0:T(8,128)(2,1)} %param.2, s32[8]{0:T(128)S(1)} %subtract_bitcast_fusion), kind=kOutput, calls=%fused_computation.66 | convolution fusion | flops 2098176 | bytes 294944 | tf_op jit(solution)/shard_map/dot_general | solution.py:28
  10.1 1.0 %collective-permute-start = (f32[8,1024]{1,0:T(8,128)S(1)}, f32[8,1024]{1,0:T(8,128)S(1)}, u32[]{:S(2)}, u32[]{:S(2)}) collective-permute-start(f32[8,1024]{1,0:T(8,128)S(1)} %fusion.56), channel_id=1, source_target_pairs={{0,4},{4,0},{8,12},{12,8},{16,20},{20,16},{24,28},{28,24},{1,5},{5... | collective-permute-start | bytes 98312 | tf_op jit(solution)/shard_map/ppermute | solution.py:31
  11.1 0.9 %collective-permute-done = f32[8,1024]{1,0:T(8,128)S(1)} collective-permute-done((f32[8,1024]{1,0:T(8,128)S(1)}, f32[8,1024]{1,0:T(8,128)S(1)}, u32[]{:S(2)}, u32[]{:S(2)}) %collective-permute-start) | collective-permute-done | bytes 32800 | tf_op jit(solution)/shard_map/ppermute | solution.py:31
  12.0 3.6 %collective-permute-start.1 = (f32[8,1024]{1,0:T(8,128)S(1)}, f32[8,1024]{1,0:T(8,128)S(1)}, u32[]{:S(2)}, u32[]{:S(2)}) collective-permute-start(f32[8,1024]{1,0:T(8,128)S(1)} %add.12), channel_id=1, source_target_pairs={{0,8},{4,12},{8,0},{12,4},{16,24},{20,28},{24,16},{28,20},{1,9},{5... | collective-permute-start | bytes 98312 | tf_op jit(solution)/shard_map/ppermute | solution.py:31
  15.6 1.9 %collective-permute-done.1 = f32[8,1024]{1,0:T(8,128)S(1)} collective-permute-done((f32[8,1024]{1,0:T(8,128)S(1)}, f32[8,1024]{1,0:T(8,128)S(1)}, u32[]{:S(2)}, u32[]{:S(2)}) %collective-permute-start.1) | collective-permute-done | bytes 32800 | tf_op jit(solution)/shard_map/ppermute | solution.py:31
  17.5 3.0 %collective-permute-start.2 = (f32[8,1024]{1,0:T(8,128)S(1)}, f32[8,1024]{1,0:T(8,128)S(1)}, u32[]{:S(2)}, u32[]{:S(2)}) collective-permute-start(f32[8,1024]{1,0:T(8,128)S(1)} %add.13), channel_id=1, source_target_pairs={{0,16},{4,20},{8,24},{12,28},{16,0},{20,4},{24,8},{28,12},{1,17},{... | collective-permute-start | bytes 98312 | tf_op jit(solution)/shard_map/ppermute | solution.py:31
  20.5 1.0 %convert_element_type.21 = f32[128,1024]{1,0:T(8,128)S(1)} convert(bf16[128,1024]{1,0:T(8,128)(2,1)} %param.2) | non-fusion elementwise | flops 131072 | bytes 786432 | tf_op jit(solution)/shard_map/convert_element_type | solution.py:34
  21.5 0.0 collective-permute-done.6
  21.5 0.1 collective-permute-start.7
  21.6 0.0 collective-permute-done.4
  21.6 0.5 collective-permute-start.5
  22.1 0.3 collective-permute-done.2
  22.4 0.1 fusion.65
  22.5 5.7 %collective-permute-done.7 = bf16[128,1024]{1,0:T(8,128)(2,1)S(1)} collective-permute-done((bf16[128,1024]{1,0:T(8,128)(2,1)S(1)}, bf16[128,1024]{1,0:T(8,128)(2,1)S(1)}, u32[]{:S(2)}, u32[]{:S(2)}) %collective-permute-start.7) | collective-permute-done | bytes 262176 | tf_op jit(solution)/shard_map/ppermute | solution.py:13
  28.3 3.7 %collective-permute-start.8 = (bf16[128,1024]{1,0:T(8,128)(2,1)S(1)}, bf16[128,1024]{1,0:T(8,128)(2,1)S(1)}, u32[]{:S(2)}, u32[]{:S(2)}) collective-permute-start(bf16[128,1024]{1,0:T(8,128)(2,1)S(1)} %collective-permute-done.7), channel_id=1, source_target_pairs={{4,0},{8,4},{12,8},{16,12},{20,16},{24,20},{28,24},{0,28},{5,1},{9... | collective-permute-start | bytes 786440 | tf_op jit(solution)/shard_map/ppermute | solution.py:13
  32.0 0.0 collective-permute-done.5
  32.0 1.0 %fusion.41 = f32[7,32,128]{2,1,0:T(8,128)S(1)} fusion(bf16[128,1024]{1,0:T(8,128)(2,1)S(1)} %collective-permute-done.5, bf16[128,1024]{1,0:T(8,128)(2,1)} %param.2, s32[]{:T(128)S(6)} %select_n.3), kind=kOutput, calls=%fused_computation.50 | convolution fusion | flops 8388607 | bytes 344068 | tf_op jit(solution)/shard_map/dot_general | solution.py:17
  33.0 1.0 %fusion.40 = f32[7,32,128]{2,1,0:T(8,128)S(1)} fusion(f32[7,32,128]{2,1,0:T(8,128)S(1)} %fusion.41, bf16[128,1024]{1,0:T(8,128)(2,1)S(1)} %collective-permute-done.4, bf16[128,1024]{1,0:T(8,128)(2,1)} %param.2, s32[]{:T(128)S(6)} %select_n.3), kind=kOutput, calls=%fused_computation.48 | convolution fusion | flops 8388608 | bytes 344068 | tf_op jit(solution)/shard_map/dot_general | solution.py:17
  34.0 1.0 %fusion.39 = f32[7,32,128]{2,1,0:T(8,128)S(1)} fusion(f32[7,32,128]{2,1,0:T(8,128)S(1)} %fusion.40, bf16[128,1024]{1,0:T(8,128)(2,1)S(1)} %collective-permute-done.3, bf16[128,1024]{1,0:T(8,128)(2,1)} %param.2, s32[]{:T(128)S(6)} %select_n.3), kind=kOutput, calls=%fused_computation.46 | convolution fusion | flops 8388608 | bytes 344068 | tf_op jit(solution)/shard_map/dot_general | solution.py:17
  35.1 1.2 %fusion.38 = f32[7,32,128]{2,1,0:T(8,128)S(1)} fusion(f32[7,32,128]{2,1,0:T(8,128)S(1)} %fusion.39, bf16[128,1024]{1,0:T(8,128)(2,1)} %param.2, s32[]{:T(128)S(6)} %select_n.3), kind=kOutput, calls=%fused_computation.44 | convolution fusion | flops 8388608 | bytes 344068 | tf_op jit(solution)/shard_map/dot_general | solution.py:17
  36.3 0.0 copy-start
  36.3 0.7 %fusion.22 = f32[7,8,128,128]{3,2,1,0:T(8,128)S(1)} fusion(f32[8,1024]{1,0:T(8,128)S(1)} %get-tuple-element.6, f32[128,1024]{1,0:T(8,128)S(1)} %convert_element_type.21, bf16[128,1024]{1,0:T(8,128)(2,1)S(1)} %collective-permute-done.5), kind=kOutput, calls=%fused_computation.24 | convolution fusion | flops 270532608 | bytes 1343488 | tf_op jit(solution)/shard_map/dot_general | solution.py:17
  37.0 0.7 %fusion.24 = f32[7,8,128,128]{3,2,1,0:T(8,128)S(1)} fusion(f32[7,8,128,128]{3,2,1,0:T(8,128)S(1)} %fusion.22, f32[8,1024]{1,0:T(8,128)S(1)} %get-tuple-element.6, f32[128,1024]{1,0:T(8,128)S(1)} %convert_element_type.21, bf16[128,1024]{1,0:T(8,128)(2,1)S(1)} %collective-permute-done.4), kind=kOutput, calls=%fused_computation.26 | convolution fusion | flops 270532608 | bytes 1343488 | tf_op jit(solution)/shard_map/dot_general | solution.py:17
  37.7 0.7 %fusion.26 = f32[7,8,128,128]{3,2,1,0:T(8,128)S(1)} fusion(f32[7,8,128,128]{3,2,1,0:T(8,128)S(1)} %fusion.24, f32[8,1024]{1,0:T(8,128)S(1)} %get-tuple-element.6, f32[128,1024]{1,0:T(8,128)S(1)} %convert_element_type.21, bf16[128,1024]{1,0:T(8,128)(2,1)S(1)} %collective-permute-done.3), kind=kOutput, calls=%fused_computation.28 | convolution fusion | flops 270532608 | bytes 1343488 | tf_op jit(solution)/shard_map/dot_general | solution.py:17
  38.5 0.0 copy-done
  38.5 0.2 fusion.37
  38.6 0.2 fusion.36
  38.8 0.7 %fusion.28 = f32[7,8,128,128]{3,2,1,0:T(8,128)S(1)} fusion(f32[7,8,128,128]{3,2,1,0:T(8,128)S(1)} %fusion.26, f32[8,1024]{1,0:T(8,128)S(1)} %get-tuple-element.6, f32[128,1024]{1,0:T(8,128)S(1)} %convert_element_type.21, bf16[128,1024]{1,0:T(8,128)(2,1)S(1)} %copy-done), kind=kOutput, calls=%fused_computation.30 | convolution fusion | flops 270532608 | bytes 1343488 | tf_op jit(solution)/shard_map/dot_general | solution.py:17
  39.6 0.0 collective-permute-done.8
  39.6 0.2 fusion.35
  39.8 9.8 %all_gather.3 = f32[7,128,128]{2,1,0:T(8,128)S(1)} all-gather(f32[7,32,128]{2,1,0:T(8,128)S(1)} %fusion.35), channel_id=1, replica_groups=mesh['vec'=8,'rep'=4] {'rep'}, dimensions={1}, use_global_device_ids=true | all-gather | bytes 573440 | tf_op jit(solution)/shard_map/all_gather | solution.py:55
  49.6 0.7 %fusion.30 = f32[7,8,128,128]{3,2,1,0:T(8,128)S(1)} fusion(f32[7,8,128,128]{3,2,1,0:T(8,128)S(1)} %fusion.28, f32[8,1024]{1,0:T(8,128)S(1)} %get-tuple-element.6, f32[128,1024]{1,0:T(8,128)S(1)} %convert_element_type.21, bf16[128,1024]{1,0:T(8,128)(2,1)S(1)} %collective-permute-done.6), kind=kOutput, calls=%fused_computation.32 | convolution fusion | flops 270532608 | bytes 1343488 | tf_op jit(solution)/shard_map/dot_general | solution.py:17
  50.3 0.7 %fusion.32 = f32[7,8,128,128]{3,2,1,0:T(8,128)S(1)} fusion(f32[7,8,128,128]{3,2,1,0:T(8,128)S(1)} %fusion.30, f32[8,1024]{1,0:T(8,128)S(1)} %get-tuple-element.6, f32[128,1024]{1,0:T(8,128)S(1)} %convert_element_type.21, bf16[128,1024]{1,0:T(8,128)(2,1)S(1)} %collective-permute-done.7), kind=kOutput, calls=%fused_computation.34 | convolution fusion | flops 270532608 | bytes 1343488 | tf_op jit(solution)/shard_map/dot_general | solution.py:17
  51.0 0.7 %fusion.34 = f32[7,8,128,128]{3,2,1,0:T(8,128)S(1)} fusion(f32[7,8,128,128]{3,2,1,0:T(8,128)S(1)} %fusion.32, f32[8,1024]{1,0:T(8,128)S(1)} %get-tuple-element.6, f32[128,1024]{1,0:T(8,128)S(1)} %convert_element_type.21, bf16[128,1024]{1,0:T(8,128)(2,1)S(1)} %collective-permute-done.8), kind=kOutput, calls=%fused_computation.36 | convolution fusion | flops 270532608 | bytes 1343488 | tf_op jit(solution)/shard_map/dot_general | solution.py:17
  51.7 1.9 %multiply_convert_fusion.8 = bf16[7,8,128,128]{3,2,1,0:T(8,128)(2,1)} fusion(f32[7,8,128,128]{3,2,1,0:T(8,128)S(1)} %fusion.34, f32[7,128,128]{2,1,0:T(8,128)S(1)} %all_gather.3, f32[8]{0:T(128)S(1)} %broadcast_multiply_fusion), kind=kLoop, calls=%fused_computation.8 | loop fusion | flops 3670016 | bytes 5963808 | tf_op jit(solution)/shard_map/convert_element_type | solution.py:59
  (3 shorter events, 0.0 us)
Async XLA Ops:
  0.0 9.0 %collective-permute-start.3 = (bf16[128,1024]{1,0:T(8,128)(2,1)}, bf16[128,1024]{1,0:T(8,128)(2,1)S(1)}, u32[]{:S(2)}, u32[]{:S(2)}) collective-permute-start(bf16[128,1024]{1,0:T(8,128)(2,1)} %param.2), channel_id=1, source_target_pairs={{28,0},{0,4},{4,8},{8,12},{12,16},{16,20},{20,24},{24,28},{29,1},{... | collective-permute-start | bytes 786440 | tf_op jit(solution)/shard_map/ppermute | solution.py:13
  0.5 21.0 %collective-permute-start.6 = (bf16[128,1024]{1,0:T(8,128)(2,1)}, bf16[128,1024]{1,0:T(8,128)(2,1)S(1)}, u32[]{:S(2)}, u32[]{:S(2)}) collective-permute-start(bf16[128,1024]{1,0:T(8,128)(2,1)} %param.2), channel_id=1, source_target_pairs={{4,0},{8,4},{12,8},{16,12},{20,16},{24,20},{28,24},{0,28},{5,1},{9... | collective-permute-start | bytes 786440 | tf_op jit(solution)/shard_map/ppermute | solution.py:13
  9.0 12.6 %collective-permute-start.4 = (bf16[128,1024]{1,0:T(8,128)(2,1)S(1)}, bf16[128,1024]{1,0:T(8,128)(2,1)S(1)}, u32[]{:S(2)}, u32[]{:S(2)}) collective-permute-start(bf16[128,1024]{1,0:T(8,128)(2,1)S(1)} %collective-permute-done.3), channel_id=1, source_target_pairs={{28,0},{0,4},{4,8},{8,12},{12,16},{16,20},{20,24},{24,28},{29,1},{... | collective-permute-start | bytes 786440 | tf_op jit(solution)/shard_map/ppermute | solution.py:13
  10.1 1.8 %collective-permute-start = (f32[8,1024]{1,0:T(8,128)S(1)}, f32[8,1024]{1,0:T(8,128)S(1)}, u32[]{:S(2)}, u32[]{:S(2)}) collective-permute-start(f32[8,1024]{1,0:T(8,128)S(1)} %fusion.56), channel_id=1, source_target_pairs={{0,4},{4,0},{8,12},{12,8},{16,20},{20,16},{24,28},{28,24},{1,5},{5... | collective-permute-start | bytes 98312 | tf_op jit(solution)/shard_map/ppermute | solution.py:31
  12.0 5.5 %collective-permute-start.1 = (f32[8,1024]{1,0:T(8,128)S(1)}, f32[8,1024]{1,0:T(8,128)S(1)}, u32[]{:S(2)}, u32[]{:S(2)}) collective-permute-start(f32[8,1024]{1,0:T(8,128)S(1)} %add.12), channel_id=1, source_target_pairs={{0,8},{4,12},{8,0},{12,4},{16,24},{20,28},{24,16},{28,20},{1,9},{5... | collective-permute-start | bytes 98312 | tf_op jit(solution)/shard_map/ppermute | solution.py:31
  17.5 4.9 %collective-permute-start.2 = (f32[8,1024]{1,0:T(8,128)S(1)}, f32[8,1024]{1,0:T(8,128)S(1)}, u32[]{:S(2)}, u32[]{:S(2)}) collective-permute-start(f32[8,1024]{1,0:T(8,128)S(1)} %add.13), channel_id=1, source_target_pairs={{0,16},{4,20},{8,24},{12,28},{16,0},{20,4},{24,8},{28,12},{1,17},{... | collective-permute-start | bytes 98312 | tf_op jit(solution)/shard_map/ppermute | solution.py:31
  21.5 6.8 %collective-permute-start.7 = (bf16[128,1024]{1,0:T(8,128)(2,1)S(1)}, bf16[128,1024]{1,0:T(8,128)(2,1)S(1)}, u32[]{:S(2)}, u32[]{:S(2)}) collective-permute-start(bf16[128,1024]{1,0:T(8,128)(2,1)S(1)} %collective-permute-done.6), channel_id=1, source_target_pairs={{4,0},{8,4},{12,8},{16,12},{20,16},{24,20},{28,24},{0,28},{5,1},{9... | collective-permute-start | bytes 786440 | tf_op jit(solution)/shard_map/ppermute | solution.py:13
  21.6 10.4 %collective-permute-start.5 = (bf16[128,1024]{1,0:T(8,128)(2,1)S(1)}, bf16[128,1024]{1,0:T(8,128)(2,1)S(1)}, u32[]{:S(2)}, u32[]{:S(2)}) collective-permute-start(bf16[128,1024]{1,0:T(8,128)(2,1)S(1)} %collective-permute-done.4), channel_id=1, source_target_pairs={{28,0},{0,4},{4,8},{8,12},{12,16},{16,20},{20,24},{24,28},{29,1},{... | collective-permute-start | bytes 786440 | tf_op jit(solution)/shard_map/ppermute | solution.py:13
  28.3 11.3 %collective-permute-start.8 = (bf16[128,1024]{1,0:T(8,128)(2,1)S(1)}, bf16[128,1024]{1,0:T(8,128)(2,1)S(1)}, u32[]{:S(2)}, u32[]{:S(2)}) collective-permute-start(bf16[128,1024]{1,0:T(8,128)(2,1)S(1)} %collective-permute-done.7), channel_id=1, source_target_pairs={{4,0},{8,4},{12,8},{16,12},{20,16},{24,20},{28,24},{0,28},{5,1},{9... | collective-permute-start | bytes 786440 | tf_op jit(solution)/shard_map/ppermute | solution.py:13
  36.3 2.2 %copy-start = (bf16[128,1024]{1,0:T(8,128)(2,1)S(1)}, bf16[128,1024]{1,0:T(8,128)(2,1)}, u32[]{:S(2)}) copy-start(bf16[128,1024]{1,0:T(8,128)(2,1)} %param.2) | copy-start | bytes 786436
